TPU v7x, 32 devices: a whole 2x2x4 slice. The times are simulated.
32 devices in a mesh: diag: 8 (over z, x), slab: 4 (over y, core).
Axes of the slice: x: 2, y: 2, z: 4, core: 2. Of those that a mesh axis runs over, the one named last changes fastest.
Arguments:
- left: float32 [8, 768, 768], P('diag', 'slab'), may hold values from -0.355756237 to 0.355756237
- right: float32 [8, 768, 768], P('diag', 'slab'), may hold values from -0.355756237 to 0.355756237
- window_a: float32 [8, 768, 768], P('diag', 'slab'), may hold values from -6 to 6
- window_b: float32 [8, 768, 768], P('diag', 'slab'), may hold values from -6 to 6
- row_slab_a: float32 [8, 512, 768], P('diag', 'slab'), may hold values from -6 to 6
- row_slab_b: float32 [8, 512, 768], P('diag', 'slab'), may hold values from -6 to 6
- column_slab_a: float32 [8, 512, 768], P('diag', 'slab'), may hold values from -6 to 6
- column_slab_b: float32 [8, 512, 768], P('diag', 'slab'), may hold values from -6 to 6
- row_live: int32 [8], P('diag'), may hold values from 256 to 512, as said below
- column_live: int32 [8], P('diag'), may hold values from 256 to 512, as said below
Outputs:
- updated_window_a: float32 [8, 768, 768], P('diag', 'slab')
- updated_window_b: float32 [8, 768, 768], P('diag', 'slab')
- updated_row_slab_a: float32 [8, 512, 768], P('diag', 'slab')
- updated_row_slab_b: float32 [8, 512, 768], P('diag', 'slab')
- updated_column_slab_a: float32 [8, 512, 768], P('diag', 'slab')
- updated_column_slab_b: float32 [8, 512, 768], P('diag', 'slab')
Inputs may be any that keep to these rules, and one draw needn't show every extreme that they name: `row_live`: in every draw one window has all 512 positions live and another exactly half of them. `column_live`: in every draw one window has all 512 positions live and another exactly half of them.
All inputs are finite; a program needn't handle non-finite values.
Results may differ from a plain program's by a relative error of at most 0.0002.
Values sent between devices are 32-bit elements; how exact they have to be, the bound alone decides.
A program may use at most 64 MiB of HBM per device.

v0:
```python
import functools

import jax
import jax.numpy as jnp
from jax import lax
from jax.experimental import pallas as pl
from jax.experimental.pallas import tpu as pltpu
from jax.sharding import PartitionSpec as P

OVL = 256
MESH = pl.DeviceIdType.MESH
F32 = jnp.float32
BF16 = jnp.bfloat16


def split(x):
    high = x.astype(BF16)
    low = (x - high.astype(F32)).astype(BF16)
    return high, low


def mm(a, b):
    return lax.dot_general(a, b, (((1,), (0,)), ((), ())), preferred_element_type=F32)


def mm3(a, b):
    return mm(a[0], b[0]) + (mm(a[0], b[1]) + mm(a[1], b[0]))


def kernel(owners, slabs, copies, *refs):
    (
        row_live, col_live, left, right, wa, wb, rsa, rsb, csa, csb,
        out_w, out_ra, out_rb, out_ca, out_cb,
        lt, rt, waf, wbf, edge_rows, slab_in, slab_out, win_out,
        part, part_in, chip_sum, other_sum, b_half,
        corner, corner_prev, b_prev, c_in, c_out, even_in, k_own, k_other,
        rt_h, rt_l, lt_h, lt_l, lp_h, lp_l,
        load_sem, own_sem, out_sem,
        send_sem, recv_sem,
    ) = refs
    d = lax.axis_index("diag")
    s = lax.axis_index("slab")
    q, c = lax.div(s, 2), lax.rem(s, 2)
    chips = slabs // 2
    mate = q * 2 + (1 - c)
    share, order = left.shape
    tiles = order // OVL
    last = tiles - 1
    cut = order - OVL
    half = OVL // 2
    kind = lax.rem(q, 2)
    odd = lax.rem(d, 2) == 1
    even = lax.rem(d, 2) == 0
    has_next = odd & (d + 2 < owners)
    has_prev = odd & (d >= 2)
    counter = iter(range(copies))

    def copy(i, src, dst, dev):
        return pltpu.make_async_remote_copy(
            src_ref=src, dst_ref=dst, send_sem=send_sem.at[i], recv_sem=recv_sem.at[i],
            device_id=dev, device_id_type=MESH)

    def chip(step):
        return lax.rem(q + step + chips, chips)

    def load(i, src, dst):
        cp = pltpu.make_async_copy(src, dst, load_sem.at[i])
        cp.start()
        return cp

    load_edge = load(0, left.at[:, pl.ds(cut, OVL)], edge_rows)
    loads = [load(1 + i, ref, slab_in.at[i]) for i, ref in enumerate((rsa, rsb, csa, csb))]

    barrier = pltpu.get_barrier_semaphore()

    def greet(dev):
        pl.semaphore_signal(barrier, inc=1, device_id=dev, device_id_type=MESH)

    pair = d + 1 - 2 * lax.rem(d, 2)
    greet((d, mate))
    for step in range(1, chips):
        greet((d, chip(step) * 2 + c))
    greet((pair, s))

    @pl.when(has_next)
    def _():
        greet((d + 2, s))

    @pl.when(has_prev)
    def _():
        greet((d - 2, s))

    sends = []

    class Gather:
        def __init__(self, index, src, buf):
            self.src, self.buf = src, buf
            self.ids = [next(counter) for _ in range(2 * chips - 1)]
            self.own = pltpu.make_async_copy(src, buf.at[s], own_sem.at[index])
            self.own.start()

        def start(self):
            for step in range(1, chips):
                cp = copy(self.ids[step], self.src, self.buf.at[s], (d, chip(step) * 2 + c))
                cp.start()
                sends.append(cp)
            cp = copy(self.ids[0], self.src, self.buf.at[s], (d, mate))
            cp.start()
            sends.append(cp)

        def relay(self):
            for step in range(1, chips):
                slot = chip(-step) * 2 + c
                copy(self.ids[step], self.src, self.buf.at[slot], (d, mate)).wait_recv()
                cp = copy(self.ids[chips + step - 1], self.buf.at[slot], self.buf.at[slot], (d, mate))
                cp.start()
                sends.append(cp)

        def finish(self, own=True):
            if own:
                self.own.wait()
            copy(self.ids[0], self.src, self.buf.at[mate], (d, mate)).wait_recv()
            for step in range(1, chips):
                slot = chip(-step) * 2 + 1 - c
                copy(self.ids[chips + step - 1], self.src, self.buf.at[slot], (d, mate)).wait_recv()

    g_wa = Gather(0, wa, waf)
    g_wb = Gather(1, wb, wbf)
    g_r = [Gather(2 + j, right.at[:, pl.ds(j * OVL, OVL)], rt.at[j]) for j in range(tiles)]
    g_l = [Gather(2 + tiles + j, left.at[:, pl.ds(j * OVL, OVL)], lt.at[j]) for j in range(tiles)]

    def tile(buf, j):
        return buf[j].reshape(order, OVL)

    pl.semaphore_wait(
        barrier, chips + 1 + has_next.astype(jnp.int32) + has_prev.astype(jnp.int32))
    g_r[last].start()
    g_l[last].start()
    g_l[0].start()
    load_edge.wait()
    own_left = split(edge_rows[...].T)
    g_wa.own.wait()
    g_wb.own.wait()
    win = [split(waf[s]), split(wbf[s])]
    g_r[last].relay()
    g_r[last].finish()
    rt_h[last], rt_l[last] = split(tile(rt, last))
    for m in range(2):
        inner = mm3(win[m], (rt_h[last], rt_l[last]))
        block = mm3(own_left, split(inner))
        part[0, m] = block[:half]
        part[1, m] = block[half:]
    i = next(counter)
    on_chip = copy(i, part.at[1 - c], part_in, (d, mate))
    on_chip.start()
    sends.append(on_chip)
    g_l[last].relay()
    on_chip.wait_recv()
    chip_sum[...] = part[c] + part_in[...]
    cross = []
    for step in range(1, chips):
        to = chip(step)
        cp = copy(next(counter), chip_sum.at[lax.rem(to, 2)], other_sum.at[step - 1], (d, to * 2 + c))
        cp.start()
        sends.append(cp)
        cross.append(cp)
    for g in g_l[1:last] + g_r[:last]:
        g.start()
    g_wa.start()
    g_wb.start()
    g_l[last].finish()
    corner[0] = tile(lt, last)[:OVL]
    corner[1] = tile(rt, last)[:OVL]
    i_corner, i_corner2, i_b, i_b2 = [next(counter) for _ in range(4)]

    def corner_copy():
        return copy(i_corner, corner.at[c], corner_prev.at[c], (pair, s))

    def b_copy():
        return copy(i_b, b_half, b_prev.at[c], (pair, s))

    @pl.when(even)
    def _():
        corner_copy().start()

    total = chip_sum[kind]
    for step in range(1, chips):
        cross[step - 1].wait_recv()
        total = total + other_sum[step - 1]
    b_half[...] = total

    @pl.when(even)
    def _():
        b_copy().start()

    i_c, i_c2, i_e, i_e2, i_k, i_k2 = [next(counter) for _ in range(6)]

    def relay_copy(i, buf):
        return copy(i, buf.at[c], buf.at[c], (d, mate))

    def relay_wait(i, buf):
        copy(i, buf.at[c], buf.at[1 - c], (d, mate)).wait_recv()

    def to_even():
        return copy(i_e, c_in.at[c], even_in.at[c], (pair, s))

    def to_next():
        return copy(i_c, c_out, c_in.at[c], (d + 2, s))

    @pl.when(odd)
    def _():
        own_left = corner[0].T
        own_left = split(jnp.where(c == 0, own_left[:half], own_left[half:]))
        own_right = split(corner[1])
        corner_copy().wait_recv()
        relay_copy(i_corner2, corner_prev).start()
        relay_wait(i_corner2, corner_prev)
        prev_left = split(corner_prev[0].T)
        prev_right = split(corner_prev[1])
        step_left = split(mm3(own_left, prev_left))
        step_right = split(mm3(prev_right, own_right))
        b_copy().wait_recv()
        relay_copy(i_b2, b_prev).start()
        relay_wait(i_b2, b_prev)
        k_own[...] = b_prev[...]
        inner = mm3(own_left, split(b_prev[...].reshape(OVL, OVL)))
        step_b = b_half[...] + mm3(split(inner), own_right)

        @pl.when(d < 2)
        def _():
            c_out[...] = step_b

        @pl.when(has_prev)
        def _():
            to_next().wait_recv()
            relay_copy(i_c2, c_in).start()
            to_even().start()
            relay_wait(i_c2, c_in)
            incoming = split(c_in[...].reshape(OVL, OVL))

            @pl.when(has_next)
            def _():
                c_out[...] = step_b + mm3(split(mm3(step_left, incoming)), step_right)
                to_next().start()

            inner = mm3(split(mm3(prev_left, incoming)), prev_right)
            k_own[...] = k_own[...] + inner.reshape(2, half, OVL)

        @pl.when(has_next & (d < 2))
        def _():
            to_next().start()

    @pl.when(d == 0)
    def _():
        k_own[...] = jnp.zeros_like(k_own)

    @pl.when(even & (d >= 2))
    def _():
        to_even().wait_recv()
        relay_copy(i_e2, even_in).start()
        relay_wait(i_e2, even_in)
        k_own[...] = even_in[...]

    k_copy = copy(i_k, k_own.at[c], k_other.at[c], (d, (q + 1 - 2 * kind) * 2 + c))
    k_copy.start()
    sends.append(k_copy)

    results = []

    def slab_pair(first, outs, live, high, low):
        n = slab_in.shape[1]
        keep = s * n + lax.broadcasted_iota(jnp.int32, (n, 1), 0) < live[0]
        for i in (first, first + 1):
            loads[i].wait()
            lhs = split(slab_in[i])
            for j in range(tiles):
                columns = slice(j * OVL, (j + 1) * OVL)
                value = mm3(lhs, (high[j], low[j]))
                slab_out[i, :, columns] = jnp.where(keep, value, slab_in[i, :, columns])
            cp = pltpu.make_async_copy(slab_out.at[i], outs[i - first], out_sem.at[i])
            cp.start()
            results.append(cp)

    for j in range(last):
        g_l[j].relay()
    for j in range(last):
        g_l[j].finish()
    for j in range(tiles):
        lt_h[j], lt_l[j] = split(tile(lt, j))
    slab_pair(0, (out_ra, out_rb), row_live, lt_h, lt_l)
    for index in range(slabs):

        @pl.when(s == index)
        def _():
            begin, end = index * share, (index + 1) * share
            low, high = begin // OVL, -(-end // OVL)
            pieces = [tile(lt, j) for j in range(low, high)]
            block = pieces[0] if len(pieces) == 1 else jnp.concatenate(pieces, axis=1)
            start = begin // 128 * 128 - low * OVL
            stop = -(-end // 128) * 128 - low * OVL
            offset = begin - low * OVL - start
            rows = block[:, start:stop].T[offset:offset + share]
            lp_h[...], lp_l[...] = split(rows)

    for j in range(last):
        g_r[j].relay()
    for j in range(last):
        g_r[j].finish()
    for j in range(last):
        rt_h[j], rt_l[j] = split(tile(rt, j))
    slab_pair(2, (out_ca, out_cb), col_live, rt_h, rt_l)

    lhs = (lp_h[...], lp_l[...])
    for m, (g, buf) in enumerate(((g_wa, waf), (g_wb, wbf))):
        g.relay()
        g.finish(own=False)
        full = buf[...].reshape(order, order)
        x = [mm3(lhs, split(full[:, j * OVL:(j + 1) * OVL])) for j in range(tiles)]
        x = split(jnp.concatenate(x, axis=1))
        for j in range(tiles):
            win_out[m, :, j * OVL:(j + 1) * OVL] = mm3(x, (rt_h[j], rt_l[j]))
    top = (lp_h[:, :OVL], lp_l[:, :OVL])

    def add_carry(m, carry):
        x = split(mm3(top, split(carry[...].reshape(OVL, OVL))))
        for j in range(tiles):
            columns = slice(j * OVL, (j + 1) * OVL)
            win_out[m, :, columns] = win_out[m, :, columns] + mm3(x, (rt_h[j, :OVL], rt_l[j, :OVL]))
        cp = pltpu.make_async_copy(win_out.at[m], out_w.at[m], out_sem.at[4 + len(results) % 2])
        cp.start()
        results.append(cp)

    add_carry(kind, k_own)
    k_copy.wait_recv()
    relay = relay_copy(i_k2, k_other)
    relay.start()
    sends.append(relay)
    relay_wait(i_k2, k_other)
    add_carry(1 - kind, k_other)
    for cp in results:
        cp.wait()

    for cp in sends:
        cp.wait_send()

    @pl.when(even)
    def _():
        corner_copy().wait_send()
        b_copy().wait_send()

    @pl.when(odd)
    def _():
        relay_copy(i_corner2, corner_prev).wait_send()
        relay_copy(i_b2, b_prev).wait_send()

    @pl.when(has_prev)
    def _():
        relay_copy(i_c2, c_in).wait_send()
        to_even().wait_send()

    @pl.when(has_next)
    def _():
        to_next().wait_send()

    @pl.when(even & (d >= 2))
    def _():
        relay_copy(i_e2, even_in).wait_send()


def write_out(*refs):
    windows, slabs, outs, held, sem = refs[0], refs[1:5], refs[5:11], refs[11:17], refs[17]
    ins = (windows.at[0], windows.at[1], *slabs)
    reads = [pltpu.make_async_copy(a, b, sem.at[0, i]) for i, (a, b) in enumerate(zip(ins, held))]
    writes = [pltpu.make_async_copy(a, b, sem.at[1, i]) for i, (a, b) in enumerate(zip(held, outs))]
    for cp in reads:
        cp.start()
    for read, write in zip(reads, writes):
        read.wait()
        write.start()
    for cp in writes:
        cp.wait()


def shards(left, right, wa, wb, rsa, rsb, csa, csb, row_live, column_live):
    owners, slabs = lax.axis_size("diag"), lax.axis_size("slab")
    chips = slabs // 2
    share, order = left.shape[1:]
    cut = order - OVL
    half = OVL // 2
    n = rsa.shape[1]
    tiles = order // OVL
    copies = (2 + 2 * tiles) * (2 * chips - 1) + 1 + (chips - 1) + 4 + 6
    smem = pl.BlockSpec(memory_space=pltpu.SMEM)
    hbm = pl.BlockSpec(memory_space=pltpu.HBM)
    win = jax.ShapeDtypeStruct((share, order), F32)
    slab = jax.ShapeDtypeStruct((n, order), F32)
    pair = pltpu.VMEM((2, half, OVL), F32)
    square = pltpu.VMEM((2, OVL, OVL), F32)
    factor = pltpu.VMEM((tiles, slabs, share, OVL), F32)
    window = pltpu.VMEM((slabs, share, order), F32)
    packed = pltpu.VMEM((tiles, order, OVL), BF16)
    outs = pl.pallas_call(
        functools.partial(kernel, owners, slabs, copies),
        out_shape=(jax.ShapeDtypeStruct((2, share, order), F32), slab, slab, slab, slab),
        in_specs=[smem] * 2 + [hbm] * 8,
        out_specs=(hbm,) * 5,
        scratch_shapes=[
            factor, factor, window, window,
            pltpu.VMEM((share, OVL), F32),
            pltpu.VMEM((4, n, order), F32),
            pltpu.VMEM((4, n, order), F32),
            pltpu.VMEM((2, share, order), F32),
            pltpu.VMEM((2, 2, half, OVL), F32),
            pair, pair,
            pltpu.VMEM((chips - 1, half, OVL), F32),
            pltpu.VMEM((half, OVL), F32),
            square, square, pair, pair,
            pltpu.VMEM((half, OVL), F32),
            pair, pair, pair,
            packed, packed, packed, packed,
            pltpu.VMEM((share, order), BF16),
            pltpu.VMEM((share, order), BF16),
            pltpu.SemaphoreType.DMA((5,)),
            pltpu.SemaphoreType.DMA((2 + 2 * tiles,)),
            pltpu.SemaphoreType.DMA((6,)),
            pltpu.SemaphoreType.DMA((copies,)),
            pltpu.SemaphoreType.DMA((copies,)),
        ],
        compiler_params=pltpu.CompilerParams(
            collective_id=0, has_side_effects=True, vmem_limit_bytes=60 * 1024 * 1024
        ),
    )(row_live, column_live, left[0], right[0], wa[0], wb[0], rsa[0], rsb[0], csa[0], csb[0])
    outs = pl.pallas_call(
        write_out,
        out_shape=(win, win, slab, slab, slab, slab),
        in_specs=[hbm] * 5,
        out_specs=(hbm,) * 6,
        scratch_shapes=[pltpu.VMEM(o.shape, F32) for o in (win, win, slab, slab, slab, slab)] + [pltpu.SemaphoreType.DMA((2, 6))],
    )(*outs)
    return tuple(o[None] for o in outs)


def solution(mesh):
    block = P("diag", "slab", None)
    return jax.shard_map(
        shards, mesh=mesh, in_specs=(block,) * 8 + (P("diag"),) * 2,
        out_specs=(block,) * 6, check_vma=False)
```

profile of v0, /device:TPU:0, one launch (start us, length us, event | category | flops | bytes accessed | tf_op | source)
XLA Modules:
  0.0 71.8 jit_solution(17117174716504966056)
XLA Ops:
  1.9 67.2 %shard_map.145 = (f32[2,192,768]{2,1,0:T(8,128)}, f32[128,768]{1,0:T(8,128)}, f32[128,768]{1,0:T(8,128)}, f32[128,768]{1,0:T(8,128)}, f32[128,768]{1,0:T(8,128)}) custom-call(s32[1]{0:T(128)S(6)} %copy.16.refs_0_, s32[1]{0:T(128)S(6)} %copy.17.refs_1_, f32[192,768]{1,0:T(8,128)} %bitcast.14, f32[192,768]{1,0:T(8,128)} %bitcast.15, f32[192,768]{1,0:T(8,128)} %bitcast.16, ...), custom_call_target="tpu_custom_call" | custom-call | tf_op jit(solution)/shard_map/pallas_call | solution.py:402
  69.2 2.7 %shard_map.146 = (f32[192,768]{1,0:T(8,128)}, f32[192,768]{1,0:T(8,128)}, f32[128,768]{1,0:T(8,128)}, f32[128,768]{1,0:T(8,128)}, f32[128,768]{1,0:T(8,128)}, /*index=5*/f32[128,768]{1,0:T(8,128)}) custom-call(f32[2,192,768]{2,1,0:T(8,128)} %get-tuple-element.17.refs_0_, f32[128,768]{1,0:T(8,128)} %get-tuple-element.18.refs_1_, ...), custom_call_target="tpu_custom_call" | custom-call | tf_op jit(solution)/shard_map/pallas_call | solution.py:433
where the time goes:
time: 72 us; the launch traced here: 71.8 us
  Pallas kernels  69.9 us (97%)
  between operations  1.93 us (3%)
    pallas_call x1, Pallas kernels, shards(): pl.pallas_call(functools.partial(kernel, owners, slabs, copies), out_shap...  67.2 us
    pallas_call x1, Pallas kernels, shards(): pl.pallas_call(write_out, out_shape=(win, win, slab, slab, slab, slab), i...  2.69 us

commit v1 on v0

--- a/solution.py
+++ b/solution.py
@@ -381,7 +381,7 @@
         cp.wait()
 
 
-def shards(left, right, wa, wb, rsa, rsb, csa, csb, row_live, column_live):
+def many_chips(left, right, wa, wb, rsa, rsb, csa, csb, row_live, column_live):
     owners, slabs = lax.axis_size("diag"), lax.axis_size("slab")
     chips = slabs // 2
     share, order = left.shape[1:]
@@ -440,8 +440,425 @@
     return tuple(o[None] for o in outs)
 
 
+def two_chip_kernel(owners, copies, *refs):
+    (
+        row_live, col_live, left, right, wa, wb, rsa, rsb, csa, csb,
+        out_w, out_s,
+        lt, rt, win, slab_in, zl, zt, p_out, p_in,
+        ends, base, base_out, trail, c_in, c_out, give, kk,
+        rt_h, rt_l, lt_h, lt_l, win_h, win_l, lx_h, lx_l, ld_h, ld_l, ll_h, ll_l, mm_h, mm_l,
+        load_sem, own_sem, send_sem, recv_sem,
+    ) = refs
+    d = lax.axis_index("diag")
+    s = lax.axis_index("slab")
+    q, c = lax.div(s, 2), lax.rem(s, 2)
+    z, x = lax.div(d, 2), lax.rem(d, 2)
+    slabs = lt.shape[1]
+    share, order = left.shape
+    tiles = order // OVL
+    last = tiles - 1
+    mate = q * 2 + (1 - c)
+    across = (1 - q) * 2 + c
+    across_mate = (1 - q) * 2 + (1 - c)
+    pair = d + 1 - 2 * x
+    mine, theirs = 1 - x, x
+    has_next = d + 2 < owners
+    has_prev = d >= 2
+    first_core = c == 0
+    counter = iter(range(copies))
+    sends, core_sends = [], []
+
+    def copy(i, src, dst, dev):
+        return pltpu.make_async_remote_copy(
+            src_ref=src, dst_ref=dst, send_sem=send_sem.at[i], recv_sem=recv_sem.at[i],
+            device_id=dev, device_id_type=MESH)
+
+    def load(i, src, dst):
+        cp = pltpu.make_async_copy(src, dst, load_sem.at[i])
+        cp.start()
+        return cp
+
+    class Gather:
+        def __init__(self, src, buf):
+            self.src, self.buf = src, buf
+            self.ids = [next(counter) for _ in range(3)]
+
+        def send(self, i, src, slot, dev):
+            cp = copy(self.ids[i], src, self.buf.at[slot], (d, dev))
+            cp.start()
+            sends.append(cp)
+
+        def wait(self, i, slot):
+            copy(self.ids[i], self.src, self.buf.at[slot], (d, mate)).wait_recv()
+
+        def to_across(self):
+            self.send(0, self.src, s, across)
+
+        def to_mate(self):
+            self.send(1, self.src, s, mate)
+
+        def relay(self):
+            self.wait(0, across)
+            self.send(2, self.buf.at[across], across, mate)
+
+        def from_mate(self):
+            self.wait(1, mate)
+
+        def relayed(self):
+            self.wait(2, across_mate)
+
+    g_r = [Gather(right.at[:, pl.ds(j * OVL, OVL)], rt.at[j]) for j in range(tiles)]
+    g_l = [Gather(left.at[:, pl.ds(j * OVL, OVL)], lt.at[j]) for j in range(tiles)]
+    g_z = [Gather(zl.at[m, s], zl.at[m]) for m in range(2)]
+    loads = [load(i, ref, win.at[i]) for i, ref in enumerate((wa, wb))]
+    own = []
+    for j in reversed(range(tiles)):
+        for i, g in ((j, g_r[j]), (tiles + j, g_l[j])):
+            cp = pltpu.make_async_copy(g.src, g.buf.at[s], own_sem.at[i])
+            cp.start()
+            own.append(cp)
+    loads += [load(2 + i, ref, slab_in.at[i]) for i, ref in enumerate((rsa, rsb, csa, csb))]
+
+    barrier = pltpu.get_barrier_semaphore()
+
+    def greet(dev):
+        pl.semaphore_signal(barrier, inc=1, device_id=dev, device_id_type=MESH)
+
+    greet((d, mate))
+    greet((d, across))
+    greet((pair, s))
+
+    @pl.when(has_next)
+    def _():
+        greet((d + 2, s))
+
+    @pl.when(has_prev)
+    def _():
+        greet((d - 2, s))
+
+    pl.semaphore_wait(barrier, 3 + has_next.astype(jnp.int32) + has_prev.astype(jnp.int32))
+    g_r[last].to_across()
+    g_l[last].to_across()
+    for g in (g_r[last], g_l[last], *g_r[:last], *g_l[:last]):
+        g.to_mate()
+
+    i_p, i_q, i_b, i_c, i_k, i_m, i_n = [next(counter) for _ in range(7)]
+    i_z = [[next(counter) for _ in range(2)] for _ in range(last)]
+    i_o = [[next(counter) for _ in range(2)] for _ in range(last)]
+
+    def end_copy(i, k):
+        return copy(i, ends.at[x, k], ends.at[x, k], (pair, s))
+
+    def end_wait(i, k):
+        copy(i, ends.at[x, k], ends.at[1 - x, k], (pair, s)).wait_recv()
+
+    def tile(buf, j):
+        return buf[j].reshape(order, OVL)
+
+    def columns(j):
+        return slice(j * OVL, (j + 1) * OVL)
+
+    def turned(begin, chip):
+        end = begin + share
+        low, high = begin // OVL, -(-end // OVL)
+        pieces = [lt[j, 2 * chip:2 * chip + 2].reshape(2 * share, OVL) for j in range(low, high)]
+        block = pieces[0] if len(pieces) == 1 else jnp.concatenate(pieces, axis=1)
+        start = begin // 128 * 128 - low * OVL
+        stop = -(-end // 128) * 128 - low * OVL
+        offset = begin - low * OVL - start
+        return split(block[:, start:stop].T[offset:offset + share])
+
+    for i in range(2):
+        loads[i].wait()
+        win_h[i], win_l[i] = split(win[i])
+    for cp in own:
+        cp.wait()
+    for g in g_l:
+        g.from_mate()
+    for index in range(slabs):
+
+        @pl.when(s == index)
+        def _():
+            chip = index // 2
+            lx_h[chip], lx_l[chip] = turned(index * share, chip)
+            ld_h[...], ld_l[...] = turned((index + 2) % slabs * share, chip)
+
+    def factor(g, buf, high, low, j):
+        g.relay()
+        g.relayed()
+        full = tile(buf, j)
+        high[j], low[j] = split(full)
+        return full
+
+    for g in g_r:
+        g.from_mate()
+    full = factor(g_r[last], rt, rt_h, rt_l, last)
+    for m in range(2):
+        zl[m, s] = mm3((win_h[m], win_l[m]), (rt_h[last], rt_l[last]))
+        g_z[m].to_across()
+        g_z[m].to_mate()
+    for g in g_r[:last] + g_l[:last]:
+        g.to_across()
+
+    @pl.when(first_core)
+    def _():
+        ends[x, 1] = rt[last].reshape(order, OVL)[:OVL]
+        end_copy(i_q, 1).start()
+
+    factor(g_l[last], lt, lt_h, lt_l, last)
+
+    @pl.when(first_core)
+    def _():
+        full = tile(lt, last)
+        ends[x, 0] = full[:OVL]
+        end_copy(i_p, 0).start()
+        ll_h[...], ll_l[...] = split(full.T)
+
+    n = slab_in.shape[1]
+    positions = s * n + lax.broadcasted_iota(jnp.int32, (n, 1), 0)
+    for i in range(4):
+        loads[2 + i].wait()
+
+    def slab_pair(first, live, high, low, j):
+        keep = positions < live[0]
+        for i in (first, first + 1):
+            value = mm3(split(slab_in[i]), (high[j], low[j]))
+            out_s[i, :, columns(j)] = jnp.where(keep, value, slab_in[i, :, columns(j)])
+
+    slab_pair(0, row_live, lt_h, lt_l, last)
+    slab_pair(2, col_live, rt_h, rt_l, last)
+
+    PE, QE, PO, QO, MT, NN = range(6)
+
+    def held(i):
+        return mm_h[i], mm_l[i]
+
+    def hold(i, value):
+        mm_h[i], mm_l[i] = split(value)
+
+    @pl.when(first_core)
+    def _():
+        end_wait(i_q, 1)
+        end_wait(i_p, 0)
+        hold(PE, ends[0, 0].T)
+        hold(QE, ends[0, 1])
+        hold(PO, ends[1, 0].T)
+        hold(QO, ends[1, 1])
+        hold(MT, mm3(held(PO), held(PE)))
+        hold(NN, mm3(held(QE), held(QO)))
+
+    for g in g_z:
+        g.relay()
+    for g in g_z:
+        g.from_mate()
+        g.relayed()
+
+    def base_copy():
+        return copy(i_b, base_out, base.at[x], (pair, s))
+
+    @pl.when(first_core)
+    def _():
+        lhs = (ll_h[...], ll_l[...])
+        base_out[...] = mm3(lhs, split(zl[theirs].reshape(order, OVL)))
+        base_copy().start()
+        base[x] = mm3(lhs, split(zl[mine].reshape(order, OVL)))
+
+    def chain_copy():
+        return copy(i_c, c_out, c_in, (d + 2, s))
+
+    def pair_copy():
+        return copy(i_k, give, kk.at[mine], (pair, s))
+
+    def mate_copy(i, m):
+        return copy(i, kk.at[m], kk.at[m], (d, mate))
+
+    def settle(incoming, inside):
+        give[...] = jnp.where(x == 1, incoming, inside)
+        kk[mine] = jnp.where(x == 1, inside, incoming)
+        pair_copy().start()
+        mate_copy(i_m, mine).start()
+
+    def chain_first():
+        @pl.when(first_core)
+        def _():
+            copy(i_b, base_out, base.at[1 - x], (pair, s)).wait_recv()
+            inner = mm3(held(PO), split(base[0]))
+            total = base[1] + mm3(split(inner), held(QO))
+            trail[...] = total
+
+            @pl.when((z == 0) & has_next)
+            def _():
+                c_out[...] = total
+                chain_copy().start()
+
+            @pl.when(z == 0)
+            def _():
+                settle(jnp.zeros_like(total), base[0])
+
+    def chain_step(when):
+        @pl.when(first_core & when)
+        def _():
+            copy(i_c, c_out, c_in, (d - 2, s)).wait_recv()
+            incoming = split(c_in[...])
+
+            @pl.when(has_next)
+            def _():
+                c_out[...] = trail[...] + mm3(held(MT), split(mm3(incoming, held(NN))))
+                chain_copy().start()
+
+            settle(c_in[...], base[0] + mm3(held(PE), split(mm3(incoming, held(QE)))))
+
+    for j in range(last):
+        factor(g_r[j], rt, rt_h, rt_l, j)
+        for m in range(2):
+            zt[j, m, c] = mm3((win_h[m], win_l[m]), (rt_h[j], rt_l[j]))
+            cp = copy(i_z[j][m], zt.at[j, m, c], zt.at[j, m, c], (d, mate))
+            cp.start()
+            sends.append(cp)
+        slab_pair(2, col_live, rt_h, rt_l, j)
+        for m in range(2):
+            copy(i_z[j][m], zt.at[j, m, c], zt.at[j, m, 1 - c], (d, mate)).wait_recv()
+        for m in range(2):
+            rhs = split(zt[j, m].reshape(2 * share, OVL))
+            p_out[j, m] = mm3((ld_h[...], ld_l[...]), rhs)
+            cp = copy(i_o[j][m], p_out.at[j, m], p_in.at[j, m], (d, across))
+            cp.start()
+            sends.append(cp)
+            out_w[m, :, columns(j)] = mm3((lx_h[q], lx_l[q]), rhs)
+        if j == 0:
+            chain_first()
+    chain_step(z == 1)
+    for j in range(last):
+        factor(g_l[j], lt, lt_h, lt_l, j)
+        slab_pair(0, row_live, lt_h, lt_l, j)
+        if j == 0:
+            chain_step(z == 2)
+    for index in range(slabs):
+
+        @pl.when(s == index)
+        def _():
+            chip = 1 - index // 2
+            lx_h[chip], lx_l[chip] = turned(index * share, chip)
+
+    for m in range(2):
+        value = [
+            mm3((lx_h[k], lx_l[k]), split(zl[m, 2 * k:2 * k + 2].reshape(2 * share, OVL)))
+            for k in range(2)
+        ]
+        out_w[m, :, columns(last)] = value[0] + value[1]
+    chain_step(z >= 3)
+
+    @pl.when(first_core)
+    def _():
+        copy(i_k, give, kk.at[theirs], (pair, s)).wait_recv()
+        mate_copy(i_n, theirs).start()
+
+    @pl.when(c == 1)
+    def _():
+        mate_copy(i_m, mine).wait_recv()
+        mate_copy(i_n, theirs).wait_recv()
+
+    top = (lx_h[0, :, :OVL], lx_l[0, :, :OVL])
+    for m in range(2):
+        value = split(mm3(top, split(kk[m])))
+        for j in range(tiles):
+            out_w[m, :, columns(j)] = (
+                out_w[m, :, columns(j)] + mm3(value, (rt_h[j, :OVL], rt_l[j, :OVL])))
+    for j in range(last):
+        for m in range(2):
+            copy(i_o[j][m], p_out.at[j, m], p_in.at[j, m], (d, across)).wait_recv()
+            out_w[m, :, columns(j)] = out_w[m, :, columns(j)] + p_in[j, m]
+
+    for cp in sends:
+        cp.wait_send()
+
+    @pl.when(first_core)
+    def _():
+        end_copy(i_q, 1).wait_send()
+        end_copy(i_p, 0).wait_send()
+        base_copy().wait_send()
+        pair_copy().wait_send()
+        mate_copy(i_m, mine).wait_send()
+        mate_copy(i_n, theirs).wait_send()
+
+        @pl.when(has_next)
+        def _():
+            chain_copy().wait_send()
+
+
+def put_out(windows, slabs, *refs):
+    outs, sem = refs[:6], refs[6]
+    held = (windows.at[0], windows.at[1], *[slabs.at[i] for i in range(4)])
+    writes = [pltpu.make_async_copy(a, b, sem.at[i]) for i, (a, b) in enumerate(zip(held, outs))]
+    for cp in writes[2:] + writes[:2]:
+        cp.start()
+    for cp in writes:
+        cp.wait()
+
+
+def two_chips(left, right, wa, wb, rsa, rsb, csa, csb, row_live, column_live):
+    owners, slabs = lax.axis_size("diag"), lax.axis_size("slab")
+    share, order = left.shape[1:]
+    n = rsa.shape[1]
+    tiles = order // OVL
+    last = tiles - 1
+    copies = 3 * (2 * tiles + 2) + 7 + 4 * last
+    smem = pl.BlockSpec(memory_space=pltpu.SMEM)
+    hbm = pl.BlockSpec(memory_space=pltpu.HBM)
+    vmem = pl.BlockSpec(memory_space=pltpu.VMEM)
+    win = jax.ShapeDtypeStruct((share, order), F32)
+    slab = jax.ShapeDtypeStruct((n, order), F32)
+    factor = pltpu.VMEM((tiles, slabs, share, OVL), F32)
+    square = pltpu.VMEM((OVL, OVL), F32)
+    squares = pltpu.VMEM((2, OVL, OVL), F32)
+    packed = pltpu.VMEM((tiles, order, OVL), BF16)
+    parts = pltpu.VMEM((last, 2, share, OVL), F32)
+    held = pl.pallas_call(
+        functools.partial(two_chip_kernel, owners, copies),
+        out_shape=(pltpu.VMEM((2, share, order), F32), pltpu.VMEM((4, n, order), F32)),
+        in_specs=[smem] * 2 + [hbm] * 8,
+        out_specs=(vmem, vmem),
+        scratch_shapes=[
+            factor, factor,
+            pltpu.VMEM((2, share, order), F32),
+            pltpu.VMEM((4, n, order), F32),
+            pltpu.VMEM((2, slabs, share, OVL), F32),
+            pltpu.VMEM((last, 2, 2, share, OVL), F32),
+            parts, parts,
+            pltpu.VMEM((2, 2, OVL, OVL), F32),
+            squares, square, square, square, square, square, squares,
+            packed, packed, packed, packed,
+            pltpu.VMEM((2, share, order), BF16), pltpu.VMEM((2, share, order), BF16),
+            pltpu.VMEM((2, share, 2 * share), BF16), pltpu.VMEM((2, share, 2 * share), BF16),
+            pltpu.VMEM((share, 2 * share), BF16), pltpu.VMEM((share, 2 * share), BF16),
+            pltpu.VMEM((OVL, order), BF16), pltpu.VMEM((OVL, order), BF16),
+            pltpu.VMEM((6, OVL, OVL), BF16), pltpu.VMEM((6, OVL, OVL), BF16),
+            pltpu.SemaphoreType.DMA((6,)),
+            pltpu.SemaphoreType.DMA((2 * tiles,)),
+            pltpu.SemaphoreType.DMA((copies,)),
+            pltpu.SemaphoreType.DMA((copies,)),
+        ],
+        compiler_params=pltpu.CompilerParams(
+            collective_id=0, has_side_effects=True, vmem_limit_bytes=44 * 1024 * 1024
+        ),
+    )(row_live, column_live, left[0], right[0], wa[0], wb[0], rsa[0], rsb[0], csa[0], csb[0])
+    outs = pl.pallas_call(
+        put_out,
+        out_shape=(win, win, slab, slab, slab, slab),
+        in_specs=[vmem] * 2,
+        out_specs=(hbm,) * 6,
+        scratch_shapes=[pltpu.SemaphoreType.DMA((6,))],
+    )(*held)
+    return tuple(o[None] for o in outs)
+
+
 def solution(mesh):
     block = P("diag", "slab", None)
+
+    def shards(*args):
+        fits = lax.axis_size("slab") == 4 and lax.axis_size("diag") % 2 == 0
+        return (two_chips if fits else many_chips)(*args)
+
     return jax.shard_map(
         shards, mesh=mesh, in_specs=(block,) * 8 + (P("diag"),) * 2,
         out_specs=(block,) * 6, check_vma=False)

time: 72 us -> 73.4 us (1.019)
  local copies, waits for them, and re-layouts: 0 us -> 10.4 us
  Pallas kernels: 69.9 us -> 60.6 us
    unnamed x0 -> x20, local copies, waits for them, and re-layouts: none -> 10.4 us
    pallas_call x2, Pallas kernels: 69.9 us -> 60.6 us  [the longest x1 57.2 us: two_chips(): pl.pallas_call(functools.partial(two_chip_kernel, owners, copies), out_sh...]
where the time goes in v1:
time: 73.4 us; the launch traced here: 72.9 us
  Pallas kernels  60.6 us (83%)
  local copies, waits for them, and re-layouts  10.4 us (14%)
  between operations  1.96 us (3%)
    pallas_call x1, Pallas kernels, two_chips(): pl.pallas_call(functools.partial(two_chip_kernel, owners, copies), out_sh...  57.2 us
    unnamed x20, local copies, waits for them, and re-layouts  10.4 us
    pallas_call x1, Pallas kernels, two_chips(): pl.pallas_call(put_out, out_shape=(win, win, slab, slab, slab, slab), in_...  3.35 us

profile of v1, /device:TPU:0, one launch (start us, length us, event | category | flops | bytes accessed | tf_op | source)
XLA Modules:
  0.0 72.9 jit_solution(7977173460851907183)
XLA Ops:
  1.9 0.0 copy-start.2
  1.9 1.1 %copy-done.2 = f32[1,192,768]{2,1,0:T(8,128)S(1)} copy-done((f32[1,192,768]{2,1,0:T(8,128)S(1)}, f32[1,192,768]{2,1,0:T(8,128)}, u32[]{:S(2)}) %copy-start.2) | copy-done | bytes 589848
  3.0 0.0 copy-start.3
  3.0 1.1 %copy-done.3 = f32[1,192,768]{2,1,0:T(8,128)S(1)} copy-done((f32[1,192,768]{2,1,0:T(8,128)S(1)}, f32[1,192,768]{2,1,0:T(8,128)}, u32[]{:S(2)}) %copy-start.3) | copy-done | bytes 589848
  4.1 0.0 copy-start.4
  4.1 1.1 %copy-done.4 = f32[1,192,768]{2,1,0:T(8,128)S(1)} copy-done((f32[1,192,768]{2,1,0:T(8,128)S(1)}, f32[1,192,768]{2,1,0:T(8,128)}, u32[]{:S(2)}) %copy-start.4) | copy-done | bytes 589848
  5.1 0.0 copy-start.5
  5.1 1.1 %copy-done.5 = f32[1,192,768]{2,1,0:T(8,128)S(1)} copy-done((f32[1,192,768]{2,1,0:T(8,128)S(1)}, f32[1,192,768]{2,1,0:T(8,128)}, u32[]{:S(2)}) %copy-start.5) | copy-done | bytes 589848
  6.2 0.0 copy-start.6
  6.2 1.0 %copy-done.6 = f32[1,128,768]{2,1,0:T(8,128)S(1)} copy-done((f32[1,128,768]{2,1,0:T(8,128)S(1)}, f32[1,128,768]{2,1,0:T(8,128)}, u32[]{:S(2)}) %copy-start.6) | copy-done | bytes 393240
  7.2 0.0 copy-start.7
  7.2 1.0 %copy-done.7 = f32[1,128,768]{2,1,0:T(8,128)S(1)} copy-done((f32[1,128,768]{2,1,0:T(8,128)S(1)}, f32[1,128,768]{2,1,0:T(8,128)}, u32[]{:S(2)}) %copy-start.7) | copy-done | bytes 393240
  8.2 0.0 copy-start.8
  8.2 1.0 %copy-done.8 = f32[1,128,768]{2,1,0:T(8,128)S(1)} copy-done((f32[1,128,768]{2,1,0:T(8,128)S(1)}, f32[1,128,768]{2,1,0:T(8,128)}, u32[]{:S(2)}) %copy-start.8) | copy-done | bytes 393240
  9.2 0.0 copy-start.9
  9.2 1.0 %copy-done.9 = f32[1,128,768]{2,1,0:T(8,128)S(1)} copy-done((f32[1,128,768]{2,1,0:T(8,128)S(1)}, f32[1,128,768]{2,1,0:T(8,128)}, u32[]{:S(2)}) %copy-start.9) | copy-done | bytes 393240
  10.2 57.2 %shard_map.145 = (f32[2,192,768]{2,1,0:T(8,128)S(1)}, f32[4,128,768]{2,1,0:T(8,128)S(1)}) custom-call(s32[1]{0:T(128)S(6)} %copy.16.refs_0_, s32[1]{0:T(128)S(6)} %copy.17.refs_1_, f32[192,768]{1,0:T(8,128)S(1)} %bitcast.14, f32[192,768]{1,0:T(8,128)S(1)} %bitcast.15, f32[192,768]{1,0:T(8,128)S(1)} %bitcast.16, f32[192,768]{1,0:T(8,128)S(1)} %bitcast.17, ...), custom_call_target="tpu_custom_call" | custom-call | tf_op jit(solution)/shard_map/pallas_call | solution.py:816
  67.4 0.0 copy-start
  67.4 1.1 %copy-done = f32[4,128,768]{2,1,0:T(8,128)} copy-done((f32[4,128,768]{2,1,0:T(8,128)}, f32[4,128,768]{2,1,0:T(8,128)S(1)}, u32[]{:S(2)}) %copy-start) | copy-done | bytes 1572888
  68.5 0.0 copy-start.1
  68.5 1.0 %copy-done.1 = f32[2,192,768]{2,1,0:T(8,128)} copy-done((f32[2,192,768]{2,1,0:T(8,128)}, f32[2,192,768]{2,1,0:T(8,128)S(1)}, u32[]{:S(2)}) %copy-start.1) | copy-done | bytes 1179672
  69.6 3.3 %shard_map.146 = (f32[192,768]{1,0:T(8,128)}, f32[192,768]{1,0:T(8,128)}, f32[128,768]{1,0:T(8,128)}, f32[128,768]{1,0:T(8,128)}, f32[128,768]{1,0:T(8,128)}, /*index=5*/f32[128,768]{1,0:T(8,128)}) custom-call(f32[2,192,768]{2,1,0:T(8,128)} %copy-done.1, f32[4,128,768]{2,1,0:T(8,128)} %copy-done), custom_call_target="tpu_custom_call" | custom-call | tf_op jit(solution)/shard_map/pallas_call | solution.py:845
Async XLA Ops:
  1.9 1.1 %copy-start.2 = (f32[1,192,768]{2,1,0:T(8,128)S(1)}, f32[1,192,768]{2,1,0:T(8,128)}, u32[]{:S(2)}) copy-start(f32[1,192,768]{2,1,0:T(8,128)} %param.10) | copy-start | bytes 1769476
  3.0 1.1 %copy-start.3 = (f32[1,192,768]{2,1,0:T(8,128)S(1)}, f32[1,192,768]{2,1,0:T(8,128)}, u32[]{:S(2)}) copy-start(f32[1,192,768]{2,1,0:T(8,128)} %param.11) | copy-start | bytes 1769476
  4.1 1.1 %copy-start.4 = (f32[1,192,768]{2,1,0:T(8,128)S(1)}, f32[1,192,768]{2,1,0:T(8,128)}, u32[]{:S(2)}) copy-start(f32[1,192,768]{2,1,0:T(8,128)} %param.12) | copy-start | bytes 1769476
  5.1 1.1 %copy-start.5 = (f32[1,192,768]{2,1,0:T(8,128)S(1)}, f32[1,192,768]{2,1,0:T(8,128)}, u32[]{:S(2)}) copy-start(f32[1,192,768]{2,1,0:T(8,128)} %param.13) | copy-start | bytes 1769476
  6.2 1.0 %copy-start.6 = (f32[1,128,768]{2,1,0:T(8,128)S(1)}, f32[1,128,768]{2,1,0:T(8,128)}, u32[]{:S(2)}) copy-start(f32[1,128,768]{2,1,0:T(8,128)} %param.14) | copy-start | bytes 1179652
  7.2 1.0 %copy-start.7 = (f32[1,128,768]{2,1,0:T(8,128)S(1)}, f32[1,128,768]{2,1,0:T(8,128)}, u32[]{:S(2)}) copy-start(f32[1,128,768]{2,1,0:T(8,128)} %param.15) | copy-start | bytes 1179652
  8.2 1.0 %copy-start.8 = (f32[1,128,768]{2,1,0:T(8,128)S(1)}, f32[1,128,768]{2,1,0:T(8,128)}, u32[]{:S(2)}) copy-start(f32[1,128,768]{2,1,0:T(8,128)} %param.16) | copy-start | bytes 1179652
  9.2 1.0 %copy-start.9 = (f32[1,128,768]{2,1,0:T(8,128)S(1)}, f32[1,128,768]{2,1,0:T(8,128)}, u32[]{:S(2)}) copy-start(f32[1,128,768]{2,1,0:T(8,128)} %param.17) | copy-start | bytes 1179652
  67.4 1.2 %copy-start = (f32[4,128,768]{2,1,0:T(8,128)}, f32[4,128,768]{2,1,0:T(8,128)S(1)}, u32[]{:S(2)}) copy-start(f32[4,128,768]{2,1,0:T(8,128)S(1)} %get-tuple-element.15.slabs) | copy-start | bytes 4718596
  68.5 1.0 %copy-start.1 = (f32[2,192,768]{2,1,0:T(8,128)}, f32[2,192,768]{2,1,0:T(8,128)S(1)}, u32[]{:S(2)}) copy-start(f32[2,192,768]{2,1,0:T(8,128)S(1)} %get-tuple-element.14.windows) | copy-start | bytes 3538948

commit v2 on v1

--- a/solution.py
+++ b/solution.py
@@ -813,6 +813,10 @@
     squares = pltpu.VMEM((2, OVL, OVL), F32)
     packed = pltpu.VMEM((tiles, order, OVL), BF16)
     parts = pltpu.VMEM((last, 2, share, OVL), F32)
+    blocks = [
+        pltpu.with_memory_space_constraint(a[0], pltpu.HBM)
+        for a in (left, right, wa, wb, rsa, rsb, csa, csb)
+    ]
     held = pl.pallas_call(
         functools.partial(two_chip_kernel, owners, copies),
         out_shape=(pltpu.VMEM((2, share, order), F32), pltpu.VMEM((4, n, order), F32)),
@@ -841,7 +845,8 @@
         compiler_params=pltpu.CompilerParams(
             collective_id=0, has_side_effects=True, vmem_limit_bytes=44 * 1024 * 1024
         ),
-    )(row_live, column_live, left[0], right[0], wa[0], wb[0], rsa[0], rsb[0], csa[0], csb[0])
+    )(row_live, column_live, *blocks)
+    held = [pltpu.with_memory_space_constraint(a, pltpu.VMEM) for a in held]
     outs = pl.pallas_call(
         put_out,
         out_shape=(win, win, slab, slab, slab, slab),

time: 73.4 us -> 60.1 us (0.82)
  local copies, waits for them, and re-layouts: 10.4 us -> 0 us
  Pallas kernels: 60.6 us -> 58 us
    unnamed x20 -> x0, local copies, waits for them, and re-layouts: 10.4 us -> none
    pallas_call x1, Pallas kernels: 3.35 us -> 1.59 us  [two_chips(): pl.pallas_call(put_out, out_shape=(win, win, slab, slab, slab, slab), in_...]
    pallas_call x1, Pallas kernels: 57.2 us -> 56.4 us  [two_chips(): pl.pallas_call(functools.partial(two_chip_kernel, owners, copies), out_sh...]
where the time goes in v2:
time: 60.1 us; the launch traced here: 59.9 us
  Pallas kernels  58 us (97%)
  between operations  1.94 us (3%)
    pallas_call x1, Pallas kernels, two_chips(): pl.pallas_call(functools.partial(two_chip_kernel, owners, copies), out_sh...  56.4 us
    pallas_call x1, Pallas kernels, two_chips(): pl.pallas_call(put_out, out_shape=(win, win, slab, slab, slab, slab), in_...  1.59 us

profile of v2, /device:TPU:0, one launch (start us, length us, event | category | flops | bytes accessed | tf_op | source)
XLA Modules:
  0.0 59.9 jit_solution(4686949519911327260)
XLA Ops:
  1.9 56.4 %shard_map.145 = (f32[2,192,768]{2,1,0:T(8,128)S(1)}, f32[4,128,768]{2,1,0:T(8,128)S(1)}) custom-call(s32[1]{0:T(128)S(6)} %copy.16.refs_0_, s32[1]{0:T(128)S(6)} %copy.17.refs_1_, f32[192,768]{1,0:T(8,128)} %bitcast.14, f32[192,768]{1,0:T(8,128)} %bitcast.15, f32[192,768]{1,0:T(8,128)} %bitcast.16, f32[192,768]{1,0:T(8,128)} %bitcast.17, ...), custom_call_target="tpu_custom_call" | custom-call | tf_op jit(solution)/shard_map/pallas_call | solution.py:820
  58.4 1.6 %shard_map.146 = (f32[192,768]{1,0:T(8,128)}, f32[192,768]{1,0:T(8,128)}, f32[128,768]{1,0:T(8,128)}, f32[128,768]{1,0:T(8,128)}, f32[128,768]{1,0:T(8,128)}, /*index=5*/f32[128,768]{1,0:T(8,128)}) custom-call(f32[2,192,768]{2,1,0:T(8,128)S(1)} %get-tuple-element.14.windows, f32[4,128,768]{2,1,0:T(8,128)S(1)} %get-tuple-element.15.slabs), custom_call_target="tpu_custom_call" | custom-call | tf_op jit(solution)/shard_map/pallas_call | solution.py:850

commit v3 on v2

--- a/solution.py
+++ b/solution.py
@@ -466,7 +466,26 @@
     has_prev = d >= 2
     first_core = c == 0
     counter = iter(range(copies))
-    sends, core_sends = [], []
+    sends = []
+    barrier = pltpu.get_barrier_semaphore()
+
+    def greet(dev):
+        pl.semaphore_signal(barrier, inc=1, device_id=dev, device_id_type=MESH)
+
+    greet((d, across))
+    greet((d, mate))
+
+    @pl.when(first_core)
+    def _():
+        greet((pair, s))
+
+    @pl.when(first_core & has_next)
+    def _():
+        greet((d + 2, s))
+
+    @pl.when(first_core & has_prev)
+    def _():
+        greet((d - 2, s))
 
     def copy(i, src, dst, dev):
         return pltpu.make_async_remote_copy(
@@ -510,6 +529,12 @@
     g_r = [Gather(right.at[:, pl.ds(j * OVL, OVL)], rt.at[j]) for j in range(tiles)]
     g_l = [Gather(left.at[:, pl.ds(j * OVL, OVL)], lt.at[j]) for j in range(tiles)]
     g_z = [Gather(zl.at[m, s], zl.at[m]) for m in range(2)]
+    around = 1 + has_next.astype(jnp.int32) + has_prev.astype(jnp.int32)
+    pl.semaphore_wait(barrier, jnp.where(first_core, 2 + around, 2))
+    g_r[last].to_across()
+    g_l[last].to_across()
+    for g in (g_r[last], g_l[last], *g_r[:last], *g_l[:last]):
+        g.to_mate()
     loads = [load(i, ref, win.at[i]) for i, ref in enumerate((wa, wb))]
     own = []
     for j in reversed(range(tiles)):
@@ -518,29 +543,6 @@
             cp.start()
             own.append(cp)
     loads += [load(2 + i, ref, slab_in.at[i]) for i, ref in enumerate((rsa, rsb, csa, csb))]
-
-    barrier = pltpu.get_barrier_semaphore()
-
-    def greet(dev):
-        pl.semaphore_signal(barrier, inc=1, device_id=dev, device_id_type=MESH)
-
-    greet((d, mate))
-    greet((d, across))
-    greet((pair, s))
-
-    @pl.when(has_next)
-    def _():
-        greet((d + 2, s))
-
-    @pl.when(has_prev)
-    def _():
-        greet((d - 2, s))
-
-    pl.semaphore_wait(barrier, 3 + has_next.astype(jnp.int32) + has_prev.astype(jnp.int32))
-    g_r[last].to_across()
-    g_l[last].to_across()
-    for g in (g_r[last], g_l[last], *g_r[:last], *g_l[:last]):
-        g.to_mate()
 
     i_p, i_q, i_b, i_c, i_k, i_m, i_n = [next(counter) for _ in range(7)]
     i_z = [[next(counter) for _ in range(2)] for _ in range(last)]
@@ -584,7 +586,6 @@
             ld_h[...], ld_l[...] = turned((index + 2) % slabs * share, chip)
 
     def factor(g, buf, high, low, j):
-        g.relay()
         g.relayed()
         full = tile(buf, j)
         high[j], low[j] = split(full)
@@ -592,7 +593,8 @@
 
     for g in g_r:
         g.from_mate()
-    full = factor(g_r[last], rt, rt_h, rt_l, last)
+    g_r[last].relay()
+    factor(g_r[last], rt, rt_h, rt_l, last)
     for m in range(2):
         zl[m, s] = mm3((win_h[m], win_l[m]), (rt_h[last], rt_l[last]))
         g_z[m].to_across()
@@ -605,6 +607,7 @@
         ends[x, 1] = rt[last].reshape(order, OVL)[:OVL]
         end_copy(i_q, 1).start()
 
+    g_l[last].relay()
     factor(g_l[last], lt, lt_h, lt_l, last)
 
     @pl.when(first_core)
@@ -616,8 +619,8 @@
 
     n = slab_in.shape[1]
     positions = s * n + lax.broadcasted_iota(jnp.int32, (n, 1), 0)
-    for i in range(4):
-        loads[2 + i].wait()
+    for cp in loads[2:]:
+        cp.wait()
 
     def slab_pair(first, live, high, low, j):
         keep = positions < live[0]
@@ -647,39 +650,41 @@
         hold(MT, mm3(held(PO), held(PE)))
         hold(NN, mm3(held(QE), held(QO)))
 
-    for g in g_z:
-        g.relay()
-    for g in g_z:
-        g.from_mate()
-        g.relayed()
-
     def base_copy():
         return copy(i_b, base_out, base.at[x], (pair, s))
 
-    @pl.when(first_core)
-    def _():
-        lhs = (ll_h[...], ll_l[...])
-        base_out[...] = mm3(lhs, split(zl[theirs].reshape(order, OVL)))
-        base_copy().start()
-        base[x] = mm3(lhs, split(zl[mine].reshape(order, OVL)))
-
     def chain_copy():
         return copy(i_c, c_out, c_in, (d + 2, s))
 
-    def pair_copy():
-        return copy(i_k, give, kk.at[mine], (pair, s))
-
-    def mate_copy(i, m):
-        return copy(i, kk.at[m], kk.at[m], (d, mate))
-
-    def settle(incoming, inside):
-        give[...] = jnp.where(x == 1, incoming, inside)
-        kk[mine] = jnp.where(x == 1, inside, incoming)
-        pair_copy().start()
-        mate_copy(i_m, mine).start()
-
-    def chain_first():
-        @pl.when(first_core)
+    def pair_copy(src):
+        return copy(i_k, src, kk.at[mine], (pair, s))
+
+    def mate_copy(i, src, m):
+        return copy(i, src, kk.at[m], (d, mate))
+
+    def share_incoming():
+        @pl.when(x == 1)
+        def _():
+            pair_copy(c_in).start()
+
+        @pl.when(x == 0)
+        def _():
+            mate_copy(i_m, c_in, mine).start()
+            kk[mine] = c_in[...]
+
+    def share_inside(inside):
+        @pl.when(x == 1)
+        def _():
+            kk[mine] = inside
+            mate_copy(i_m, kk.at[mine], mine).start()
+
+        @pl.when(x == 0)
+        def _():
+            give[...] = inside
+            pair_copy(give).start()
+
+    def chain_first(when):
+        @pl.when(first_core & when)
         def _():
             copy(i_b, base_out, base.at[1 - x], (pair, s)).wait_recv()
             inner = mm3(held(PO), split(base[0]))
@@ -693,12 +698,15 @@
 
             @pl.when(z == 0)
             def _():
-                settle(jnp.zeros_like(total), base[0])
+                c_in[...] = jnp.zeros_like(total)
+                share_incoming()
+                share_inside(base[0])
 
     def chain_step(when):
         @pl.when(first_core & when)
         def _():
             copy(i_c, c_out, c_in, (d - 2, s)).wait_recv()
+            share_incoming()
             incoming = split(c_in[...])
 
             @pl.when(has_next)
@@ -706,15 +714,39 @@
                 c_out[...] = trail[...] + mm3(held(MT), split(mm3(incoming, held(NN))))
                 chain_copy().start()
 
-            settle(c_in[...], base[0] + mm3(held(PE), split(mm3(incoming, held(QE)))))
-
+            share_inside(base[0] + mm3(held(PE), split(mm3(incoming, held(QE)))))
+
+    for m in range(2):
+        g_z[m].relay()
+        g_z[m].from_mate()
+        g_z[m].relayed()
+
+        @pl.when(first_core)
+        def _():
+            value = mm3((ll_h[...], ll_l[...]), split(zl[m].reshape(order, OVL)))
+
+            @pl.when(theirs == m)
+            def _():
+                base_out[...] = value
+                base_copy().start()
+
+            @pl.when(mine == m)
+            def _():
+                base[x] = value
+
+    chain_first(x == 1)
     for j in range(last):
+        g_r[j].relay()
         factor(g_r[j], rt, rt_h, rt_l, j)
         for m in range(2):
             zt[j, m, c] = mm3((win_h[m], win_l[m]), (rt_h[j], rt_l[j]))
             cp = copy(i_z[j][m], zt.at[j, m, c], zt.at[j, m, c], (d, mate))
             cp.start()
             sends.append(cp)
+        if j == 0:
+            chain_first(x == 0)
+        if j == last - 1:
+            chain_step((x == 0) & (z == 1))
         slab_pair(2, col_live, rt_h, rt_l, j)
         for m in range(2):
             copy(i_z[j][m], zt.at[j, m, c], zt.at[j, m, 1 - c], (d, mate)).wait_recv()
@@ -726,13 +758,14 @@
             sends.append(cp)
             out_w[m, :, columns(j)] = mm3((lx_h[q], lx_l[q]), rhs)
         if j == 0:
-            chain_first()
-    chain_step(z == 1)
+            chain_step((x == 1) & (z == 1))
+    chain_step((x == 1) & (z == 2))
     for j in range(last):
+        g_l[j].relay()
         factor(g_l[j], lt, lt_h, lt_l, j)
         slab_pair(0, row_live, lt_h, lt_l, j)
         if j == 0:
-            chain_step(z == 2)
+            chain_step(((x == 1) & (z == 3)) | ((x == 0) & (z == 2)))
     for index in range(slabs):
 
         @pl.when(s == index)
@@ -746,17 +779,17 @@
             for k in range(2)
         ]
         out_w[m, :, columns(last)] = value[0] + value[1]
-    chain_step(z >= 3)
+    chain_step(((x == 1) & (z > 3)) | ((x == 0) & (z >= 3)))
 
     @pl.when(first_core)
     def _():
         copy(i_k, give, kk.at[theirs], (pair, s)).wait_recv()
-        mate_copy(i_n, theirs).start()
+        mate_copy(i_n, kk.at[theirs], theirs).start()
 
     @pl.when(c == 1)
     def _():
-        mate_copy(i_m, mine).wait_recv()
-        mate_copy(i_n, theirs).wait_recv()
+        mate_copy(i_m, give, mine).wait_recv()
+        mate_copy(i_n, give, theirs).wait_recv()
 
     top = (lx_h[0, :, :OVL], lx_l[0, :, :OVL])
     for m in range(2):
@@ -777,9 +810,9 @@
         end_copy(i_q, 1).wait_send()
         end_copy(i_p, 0).wait_send()
         base_copy().wait_send()
-        pair_copy().wait_send()
-        mate_copy(i_m, mine).wait_send()
-        mate_copy(i_n, theirs).wait_send()
+        pair_copy(give).wait_send()
+        mate_copy(i_m, give, mine).wait_send()
+        mate_copy(i_n, give, theirs).wait_send()
 
         @pl.when(has_next)
         def _():
@@ -803,7 +836,6 @@
     tiles = order // OVL
     last = tiles - 1
     copies = 3 * (2 * tiles + 2) + 7 + 4 * last
-    smem = pl.BlockSpec(memory_space=pltpu.SMEM)
     hbm = pl.BlockSpec(memory_space=pltpu.HBM)
     vmem = pl.BlockSpec(memory_space=pltpu.VMEM)
     win = jax.ShapeDtypeStruct((share, order), F32)
@@ -820,7 +852,7 @@
     held = pl.pallas_call(
         functools.partial(two_chip_kernel, owners, copies),
         out_shape=(pltpu.VMEM((2, share, order), F32), pltpu.VMEM((4, n, order), F32)),
-        in_specs=[smem] * 2 + [hbm] * 8,
+        in_specs=[pl.BlockSpec(memory_space=pltpu.SMEM)] * 2 + [hbm] * 8,
         out_specs=(vmem, vmem),
         scratch_shapes=[
             factor, factor,

time: 60.1 us -> 59.4 us (0.988)
  Pallas kernels: 58 us -> 57.1 us
    pallas_call x1, Pallas kernels: 56.4 us -> 55.5 us  [two_chips(): pl.pallas_call(functools.partial(two_chip_kernel, owners, copies), out_sh...]
where the time goes in v3:
time: 59.4 us; the launch traced here: 59.2 us
  Pallas kernels  57.1 us (96%)
  between operations  2.1 us (4%)
    pallas_call x1, Pallas kernels, two_chips(): pl.pallas_call(functools.partial(two_chip_kernel, owners, copies), out_sh...  55.5 us
    pallas_call x1, Pallas kernels, two_chips(): pl.pallas_call(put_out, out_shape=(win, win, slab, slab, slab, slab), in_...  1.59 us

profile of v3, /device:TPU:0, one launch (start us, length us, event | category | flops | bytes accessed | tf_op | source)
XLA Modules:
  0.0 59.2 jit_solution(15678217201642567294)
XLA Ops:
  1.9 55.5 %shard_map.145 = (f32[2,192,768]{2,1,0:T(8,128)S(1)}, f32[4,128,768]{2,1,0:T(8,128)S(1)}) custom-call(s32[1]{0:T(128)S(6)} %copy.16.refs_0_, s32[1]{0:T(128)S(6)} %copy.17.refs_1_, f32[192,768]{1,0:T(8,128)} %bitcast.14, f32[192,768]{1,0:T(8,128)} %bitcast.15, f32[192,768]{1,0:T(8,128)} %bitcast.16, f32[192,768]{1,0:T(8,128)} %bitcast.17, ...), custom_call_target="tpu_custom_call" | custom-call | tf_op jit(solution)/shard_map/pallas_call | solution.py:852
  57.5 1.6 %shard_map.146 = (f32[192,768]{1,0:T(8,128)}, f32[192,768]{1,0:T(8,128)}, f32[128,768]{1,0:T(8,128)}, f32[128,768]{1,0:T(8,128)}, f32[128,768]{1,0:T(8,128)}, /*index=5*/f32[128,768]{1,0:T(8,128)}) custom-call(f32[2,192,768]{2,1,0:T(8,128)S(1)} %get-tuple-element.14.windows, f32[4,128,768]{2,1,0:T(8,128)S(1)} %get-tuple-element.15.slabs), custom_call_target="tpu_custom_call" | custom-call | tf_op jit(solution)/shard_map/pallas_call | solution.py:882
